TPU v7x, 128 devices: a whole 4x4x4 slice. The times are simulated.
128 devices in a mesh: dom: 128 (over x, z, y, core).
Axes of the slice: x: 4, y: 4, z: 4, core: 2. Of those that a mesh axis runs over, the one named last changes fastest.
Arguments:
- rhs_fields: float32 [64, 524288], P(None, 'dom')
- diag_blocks: float32 [4096, 128, 128], P('dom')
- off_blocks: float32 [4096, 3, 128, 128], P('dom')
- block_cols: int32 [4096, 3], P('dom'), may hold values from 0 to 39, as said below
- send_lists: int32 [128, 2, 4], P('dom'), may hold values from 0 to 31, as said below
- fine_agg: int32 [524288], P('dom'), may hold values from 0 to 127, as said below
- coarse_diag: float32 [128, 128, 128], P('dom')
- coarse_side: float32 [128, 2, 128, 128], P('dom')
- coarse_agg: int32 [16384], P('dom'), may hold values from 0 to 7, as said below
- coarse_inverse: float32 [1024, 1024], replicated
Outputs:
- solution: float32 [64, 524288], P(None, 'dom')
Inputs may be any that keep to these rules, and one draw needn't show every extreme that they name: `block_cols`: entries below 32 name own block rows, 32 to 35 the lower neighbour's sent blocks, the rest the upper neighbour's; every sent slot is named by some block row of the receiving partition. `send_lists`: the 4 entries of each list are distinct local block rows. `fine_agg`: every aggregate of every partition holds at least one node. `coarse_agg`: every second-level aggregate of every partition holds at least one coarse node.
All inputs are finite; a program needn't handle non-finite values.
Results may differ from a plain program's by a relative error of at most 0.0001.
Values sent between devices are 32-bit elements; how exact they have to be, the bound alone decides.
A program may use at most 128 MiB of HBM per device.

v0:
```python
import jax
import jax.numpy as jnp
from jax import lax
from jax.sharding import PartitionSpec as P

SWEEPS = 2
CYCLES = 2


relax_weight = 0.6
smooth_weight = 0.5


def from_behind(value, axis, steps):
    count = lax.axis_size(axis)
    pairs = [(source, (source + steps) % count) for source in range(count)]
    return lax.ppermute(value, axis, pairs)


def local(
    rhs_fields,
    diag_blocks,
    off_blocks,
    block_cols,
    send_lists,
    fine_agg,
    coarse_diag,
    coarse_side,
    coarse_agg,
    coarse_inverse,
):
    hp = lax.Precision.HIGHEST
    nrows = diag_blocks.shape[0]
    width = diag_blocks.shape[1]
    nright = rhs_fields.shape[0]
    naggs = coarse_diag.shape[1]
    nsecond = coarse_inverse.shape[0] // lax.axis_size("dom")
    lists = send_lists[0]

    def fine_op(field):
        blocks_view = field.reshape(nright, nrows, width)
        to_upper = blocks_view[:, lists[1], :]
        to_lower = blocks_view[:, lists[0], :]
        from_lower = from_behind(to_upper, "dom", 1)
        from_upper = from_behind(to_lower, "dom", -1)
        result = jnp.einsum("iab,rib->ria", diag_blocks, blocks_view, precision=hp)
        extended = jnp.concatenate([blocks_view, from_lower, from_upper], axis=1)
        picked = extended[:, block_cols, :]
        result = result + jnp.einsum("ikab,rikb->ria", off_blocks, picked, precision=hp)
        return result.reshape(nright, nrows * width)

    def coarse_op(field):
        below = from_behind(field, "dom", 1)
        above = from_behind(field, "dom", -1)
        result = jnp.dot(field, coarse_diag[0].T, precision=hp)
        result = result + jnp.dot(below, coarse_side[0, 0].T, precision=hp)
        return result + jnp.dot(above, coarse_side[0, 1].T, precision=hp)

    dinv = 1.0 / jnp.diagonal(diag_blocks, axis1=1, axis2=2).reshape(nrows * width)
    d1inv = 1.0 / jnp.diagonal(coarse_diag[0])
    table_one = (fine_agg[:, None] == jnp.arange(naggs, dtype=jnp.int32)[None, :]).astype(
        jnp.float32
    )
    scale_one = 1.0 / jnp.sqrt(jnp.sum(table_one, axis=0))
    table_two = (coarse_agg[:, None] == jnp.arange(nsecond, dtype=jnp.int32)[None, :]).astype(
        jnp.float32
    )
    scale_two = 1.0 / jnp.sqrt(jnp.sum(table_two, axis=0))
    offset = lax.axis_index("dom") * nsecond
    solution = jnp.zeros_like(rhs_fields)
    for cycle_index in range(CYCLES):
        for sweep_index in range(SWEEPS):
            solution = solution + relax_weight * dinv * (rhs_fields - fine_op(solution))
        resid = rhs_fields - fine_op(solution)
        smoothed = resid - smooth_weight * fine_op(dinv * resid)
        right_one = jnp.dot(smoothed, table_one, precision=hp) * scale_one
        iterate = jnp.zeros((nright, naggs), jnp.float32)
        for coarse_sweep_index in range(SWEEPS):
            iterate = iterate + relax_weight * d1inv * (right_one - coarse_op(iterate))
        resid_one = right_one - coarse_op(iterate)
        coarse_resid_two = jnp.dot(resid_one, table_two, precision=hp) * scale_two
        gathered = lax.all_gather(coarse_resid_two, "dom", axis=1, tiled=True)
        own_rows = lax.dynamic_slice_in_dim(coarse_inverse, offset, nsecond, 0)
        correction = jnp.dot(gathered, own_rows.T, precision=hp)
        iterate = iterate + jnp.dot(correction * scale_two, table_two.T, precision=hp)
        for coarse_sweep_index in range(SWEEPS):
            iterate = iterate + relax_weight * d1inv * (right_one - coarse_op(iterate))
        lifted = jnp.dot(iterate * scale_one, table_one.T, precision=hp)
        solution = solution + lifted - smooth_weight * dinv * fine_op(lifted)
        for sweep_index in range(SWEEPS):
            solution = solution + relax_weight * dinv * (rhs_fields - fine_op(solution))
    return solution


def solution(mesh):
    return jax.shard_map(
        local,
        mesh=mesh,
        in_specs=(
            P(None, "dom"),
            P("dom", None, None),
            P("dom", None, None, None),
            P("dom", None),
            P("dom", None, None),
            P("dom"),
            P("dom", None, None),
            P("dom", None, None, None),
            P("dom"),
            P(),
        ),
        out_specs=P(None, "dom"),
        check_vma=False,
    )
```

profile of v0, /device:TPU:0, one launch (start us, length us, event | category | flops | bytes accessed | tf_op | source)
XLA Modules:
  0.0 716.4 jit_solution(1109189247107197619)
XLA Ops:
  0.0 8.4 %collective-permute-start.9 = (f32[64,128]{1,0:T(8,128)S(1)}, f32[64,128]{1,0:T(8,128)S(1)}, u32[]{:S(2)}, u32[]{:S(2)}) collective-permute-start(f32[64,128]{1,0:T(8,128)S(1)} %broadcast.115), channel_id=1, source_target_pairs={{0,127},{1,0},{2,1},{3,2},{4,3},{5,4},{6,5},{7,6},{8,7},{9,8},{10,... | collective-permute-start | bytes 98312 | tf_op jit(solution)/shard_map/ppermute | solution.py:17
  35.5 12.8 %fusion.33 = f32[32,8,8,128]{3,2,1,0:T(8,128)S(1)} fusion(f32[32,64,128]{2,1,0:T(8,128)} %fusion.82, f32[64,32,3,128]{3,0,2,1:T(8,128)} %bitcast.591, f32[32,3,128,128]{3,2,1,0:T(8,128)} %param.12), kind=kOutput, calls=%fused_computation.93 | convolution fusion | flops 1208221696 | bytes 11534336 | tf_op jit(solution)/shard_map/ikab,rikb->ria/dot_general | solution.py:49
  77.8 12.8 %fusion.31 = f32[32,8,8,128]{3,2,1,0:T(8,128)S(1)} fusion(f32[32,64,128]{2,1,0:T(8,128)} %fusion.154, f32[64,32,3,128]{3,0,2,1:T(8,128)} %bitcast.592, f32[32,3,128,128]{3,2,1,0:T(8,128)} %param.12), kind=kOutput, calls=%fused_computation.90 | convolution fusion | flops 1208221696 | bytes 11534336 | tf_op jit(solution)/shard_map/ikab,rikb->ria/dot_general | solution.py:49
  116.4 12.7 %fusion.29 = f32[32,8,8,128]{3,2,1,0:T(8,128)S(1)} fusion(f32[32,64,128]{2,1,0:T(8,128)} %fusion.155, f32[64,32,3,128]{3,0,2,1:T(8,128)} %bitcast.593, f32[32,3,128,128]{3,2,1,0:T(8,128)} %param.12), kind=kOutput, calls=%fused_computation.87 | convolution fusion | flops 1208221696 | bytes 11534336 | tf_op jit(solution)/shard_map/ikab,rikb->ria/dot_general | solution.py:49
  154.7 12.8 %fusion.27 = f32[32,8,8,128]{3,2,1,0:T(8,128)S(1)} fusion(f32[32,64,128]{2,1,0:T(8,128)} %fusion.156, f32[64,32,3,128]{3,0,2,1:T(8,128)} %bitcast.594, f32[32,3,128,128]{3,2,1,0:T(8,128)} %param.12), kind=kOutput, calls=%fused_computation.84 | convolution fusion | flops 1208483840 | bytes 11534336 | tf_op jit(solution)/shard_map/ikab,rikb->ria/dot_general | solution.py:49
  168.9 7.2 %collective-permute-start.11 = (f32[64,128]{1,0:T(8,128)S(1)}, f32[64,128]{1,0:T(8,128)S(1)}, u32[]{:S(2)}, u32[]{:S(2)}) collective-permute-start(f32[64,128]{1,0:T(8,128)S(1)} %get-tuple-element.9), channel_id=1, source_target_pairs={{0,127},{1,0},{2,1},{3,2},{4,3},{5,4},{6,5},{7,6},{8,7},{9,8},{10,... | collective-permute-start | bytes 98312 | tf_op jit(solution)/shard_map/ppermute | solution.py:17
  178.7 7.2 %collective-permute-start.13 = (f32[64,128]{1,0:T(8,128)S(1)}, f32[64,128]{1,0:T(8,128)S(1)}, u32[]{:S(2)}, u32[]{:S(2)}) collective-permute-start(f32[64,128]{1,0:T(8,128)S(1)} %fusion.57), channel_id=1, source_target_pairs={{0,127},{1,0},{2,1},{3,2},{4,3},{5,4},{6,5},{7,6},{8,7},{9,8},{10,... | collective-permute-start | bytes 98312 | tf_op jit(solution)/shard_map/ppermute | solution.py:17
  187.9 36.1 %all_gather.6 = f32[64,1024]{0,1:T(8,128)S(1)} all-gather(f32[64,8]{0,1:T(8,128)S(1)} %convolution_multiply_fusion.1), channel_id=1, replica_groups=mesh['dom'=128] {'dom'}, dimensions={1}, use_global_device_ids=true | all-gather | bytes 264192 | tf_op jit(solution)/shard_map/all_gather | solution.py:82
  235.1 7.2 %collective-permute-start.17 = (f32[64,128]{1,0:T(8,128)S(1)}, f32[64,128]{1,0:T(8,128)S(1)}, u32[]{:S(2)}, u32[]{:S(2)}) collective-permute-start(f32[64,128]{1,0:T(8,128)S(1)} %fusion.53), channel_id=1, source_target_pairs={{0,127},{1,0},{2,1},{3,2},{4,3},{5,4},{6,5},{7,6},{8,7},{9,8},{10,... | collective-permute-start | bytes 98312 | tf_op jit(solution)/shard_map/ppermute | solution.py:17
  253.3 7.2 %collective-permute-start.19 = (f32[64,4,128]{2,0,1:T(8,128)}, f32[64,4,128]{2,0,1:T(8,128)S(1)}, u32[]{:S(2)}, u32[]{:S(2)}) collective-permute-start(f32[64,4,128]{2,0,1:T(8,128)} %bitcast.628), channel_id=1, source_target_pairs={{0,127},{1,0},{2,1},{3,2},{4,3},{5,4},{6,5},{7,6},{8,7},{9,8},{10,... | collective-permute-start | bytes 393224 | tf_op jit(solution)/shard_map/ppermute | solution.py:17
  275.6 12.9 %fusion.24 = f32[32,8,8,128]{3,2,1,0:T(8,128)S(1)} fusion(f32[32,64,128]{2,1,0:T(8,128)} %fusion.157, f32[64,32,3,128]{3,0,2,1:T(8,128)} %bitcast.595, f32[32,3,128,128]{3,2,1,0:T(8,128)} %param.12), kind=kOutput, calls=%fused_computation.80 | convolution fusion | flops 1208221696 | bytes 11534336 | tf_op jit(solution)/shard_map/ikab,rikb->ria/dot_general | solution.py:49
  314.2 12.8 %fusion.22 = f32[32,8,8,128]{3,2,1,0:T(8,128)S(1)} fusion(f32[32,64,128]{2,1,0:T(8,128)} %fusion.158, f32[64,32,3,128]{3,0,2,1:T(8,128)} %bitcast.596, f32[32,3,128,128]{3,2,1,0:T(8,128)} %param.12), kind=kOutput, calls=%fused_computation.77 | convolution fusion | flops 1208221696 | bytes 11534336 | tf_op jit(solution)/shard_map/ikab,rikb->ria/dot_general | solution.py:49
  352.8 12.9 %fusion.20 = f32[32,8,8,128]{3,2,1,0:T(8,128)S(1)} fusion(f32[32,64,128]{2,1,0:T(8,128)} %fusion.159, f32[64,32,3,128]{3,0,2,1:T(8,128)} %bitcast.597, f32[32,3,128,128]{3,2,1,0:T(8,128)} %param.12), kind=kOutput, calls=%fused_computation.74 | convolution fusion | flops 1208221696 | bytes 11534336 | tf_op jit(solution)/shard_map/ikab,rikb->ria/dot_general | solution.py:49
  391.8 12.8 %fusion.18 = f32[32,8,8,128]{3,2,1,0:T(8,128)S(1)} fusion(f32[32,64,128]{2,1,0:T(8,128)} %fusion.160, f32[64,32,3,128]{3,0,2,1:T(8,128)} %bitcast.598, f32[32,3,128,128]{3,2,1,0:T(8,128)} %param.12), kind=kOutput, calls=%fused_computation.71 | convolution fusion | flops 1208221696 | bytes 11534336 | tf_op jit(solution)/shard_map/ikab,rikb->ria/dot_general | solution.py:49
  430.3 12.9 %fusion.16 = f32[32,8,8,128]{3,2,1,0:T(8,128)S(1)} fusion(f32[32,64,128]{2,1,0:T(8,128)} %fusion.161, f32[64,32,3,128]{3,0,2,1:T(8,128)} %bitcast.599, f32[32,3,128,128]{3,2,1,0:T(8,128)} %param.12), kind=kOutput, calls=%fused_computation.68 | convolution fusion | flops 1208221696 | bytes 11534336 | tf_op jit(solution)/shard_map/ikab,rikb->ria/dot_general | solution.py:49
  469.5 12.7 %fusion.14 = f32[32,8,8,128]{3,2,1,0:T(8,128)S(1)} fusion(f32[32,64,128]{2,1,0:T(8,128)} %fusion.162, f32[64,32,3,128]{3,0,2,1:T(8,128)} %bitcast.600, f32[32,3,128,128]{3,2,1,0:T(8,128)} %param.12), kind=kOutput, calls=%fused_computation.65 | convolution fusion | flops 1208221696 | bytes 11534336 | tf_op jit(solution)/shard_map/ikab,rikb->ria/dot_general | solution.py:49
  507.8 12.8 %fusion.12 = f32[32,8,8,128]{3,2,1,0:T(8,128)S(1)} fusion(f32[32,64,128]{2,1,0:T(8,128)} %fusion.163, f32[64,32,3,128]{3,0,2,1:T(8,128)} %bitcast.601, f32[32,3,128,128]{3,2,1,0:T(8,128)} %param.12), kind=kOutput, calls=%fused_computation.62 | convolution fusion | flops 1208483840 | bytes 11534336 | tf_op jit(solution)/shard_map/ikab,rikb->ria/dot_general | solution.py:49
  522.0 7.2 %collective-permute-start.33 = (f32[64,128]{1,0:T(8,128)S(1)}, f32[64,128]{1,0:T(8,128)S(1)}, u32[]{:S(2)}, u32[]{:S(2)}) collective-permute-start(f32[64,128]{1,0:T(8,128)S(1)} %get-tuple-element.11), channel_id=1, source_target_pairs={{0,127},{1,0},{2,1},{3,2},{4,3},{5,4},{6,5},{7,6},{8,7},{9,8},{10,... | collective-permute-start | bytes 98312 | tf_op jit(solution)/shard_map/ppermute | solution.py:17
  531.6 7.2 %collective-permute-start.35 = (f32[64,128]{1,0:T(8,128)S(1)}, f32[64,128]{1,0:T(8,128)S(1)}, u32[]{:S(2)}, u32[]{:S(2)}) collective-permute-start(f32[64,128]{1,0:T(8,128)S(1)} %fusion.46), channel_id=1, source_target_pairs={{0,127},{1,0},{2,1},{3,2},{4,3},{5,4},{6,5},{7,6},{8,7},{9,8},{10,... | collective-permute-start | bytes 98312 | tf_op jit(solution)/shard_map/ppermute | solution.py:17
  540.8 36.1 %all_gather.7 = f32[64,1024]{0,1:T(8,128)S(1)} all-gather(f32[64,8]{0,1:T(8,128)S(1)} %convolution_multiply_fusion), channel_id=1, replica_groups=mesh['dom'=128] {'dom'}, dimensions={1}, use_global_device_ids=true | all-gather | bytes 264192 | tf_op jit(solution)/shard_map/all_gather | solution.py:82
  588.0 7.2 %collective-permute-start.39 = (f32[64,128]{1,0:T(8,128)S(1)}, f32[64,128]{1,0:T(8,128)S(1)}, u32[]{:S(2)}, u32[]{:S(2)}) collective-permute-start(f32[64,128]{1,0:T(8,128)S(1)} %fusion.42), channel_id=1, source_target_pairs={{0,127},{1,0},{2,1},{3,2},{4,3},{5,4},{6,5},{7,6},{8,7},{9,8},{10,... | collective-permute-start | bytes 98312 | tf_op jit(solution)/shard_map/ppermute | solution.py:17
  628.7 12.9 %fusion.9 = f32[32,8,8,128]{3,2,1,0:T(8,128)S(1)} fusion(f32[32,64,128]{2,1,0:T(8,128)} %fusion.164, f32[64,32,3,128]{3,0,2,1:T(8,128)} %bitcast.602, f32[32,3,128,128]{3,2,1,0:T(8,128)} %param.12), kind=kOutput, calls=%fused_computation.58 | convolution fusion | flops 1208221696 | bytes 11534336 | tf_op jit(solution)/shard_map/ikab,rikb->ria/dot_general | solution.py:49
  666.5 12.8 %fusion.7 = f32[32,8,8,128]{3,2,1,0:T(8,128)S(1)} fusion(f32[32,64,128]{2,1,0:T(8,128)} %fusion.165, f32[64,32,3,128]{3,0,2,1:T(8,128)} %bitcast.603, f32[32,3,128,128]{3,2,1,0:T(8,128)} %param.12), kind=kOutput, calls=%fused_computation.55 | convolution fusion | flops 1208221696 | bytes 11534336 | tf_op jit(solution)/shard_map/ikab,rikb->ria/dot_general | solution.py:49
  702.0 12.9 %fusion.5 = f32[32,8,8,128]{3,2,1,0:T(8,128)S(1)} fusion(f32[32,64,128]{2,1,0:T(8,128)} %fusion.166, f32[64,32,3,128]{3,0,2,1:T(8,128)} %bitcast.590, f32[32,3,128,128]{3,2,1,0:T(8,128)} %param.12), kind=kOutput, calls=%fused_computation.52 | convolution fusion | flops 1208221696 | bytes 11534336 | tf_op jit(solution)/shard_map/ikab,rikb->ria/dot_general | solution.py:49
  (330 shorter events, 404.3 us)
Async XLA Ops:
  0.0 28.8 %collective-permute-start.8 = (f32[64,128]{1,0:T(8,128)S(1)}, f32[64,128]{1,0:T(8,128)S(1)}, u32[]{:S(2)}, u32[]{:S(2)}) collective-permute-start(f32[64,128]{1,0:T(8,128)S(1)} %broadcast.115), channel_id=1, source_target_pairs={{0,1},{1,2},{2,3},{3,4},{4,5},{5,6},{6,7},{7,8},{8,9},{9,10},{10,1... | collective-permute-start | bytes 98312 | tf_op jit(solution)/shard_map/ppermute | solution.py:17
  0.0 29.1 %collective-permute-start.9 = (f32[64,128]{1,0:T(8,128)S(1)}, f32[64,128]{1,0:T(8,128)S(1)}, u32[]{:S(2)}, u32[]{:S(2)}) collective-permute-start(f32[64,128]{1,0:T(8,128)S(1)} %broadcast.115), channel_id=1, source_target_pairs={{0,127},{1,0},{2,1},{3,2},{4,3},{5,4},{6,5},{7,6},{8,7},{9,8},{10,... | collective-permute-start | bytes 98312 | tf_op jit(solution)/shard_map/ppermute | solution.py:17
  9.8 19.5 %collective-permute-start.1 = (f32[64,4,128]{2,0,1:T(8,128)S(1)}, f32[64,4,128]{2,0,1:T(8,128)S(1)}, u32[]{:S(2)}, u32[]{:S(2)}) collective-permute-start(f32[64,4,128]{2,0,1:T(8,128)S(1)} %bitcast.608), channel_id=1, source_target_pairs={{0,127},{1,0},{2,1},{3,2},{4,3},{5,4},{6,5},{7,6},{8,7},{9,8},{10,... | collective-permute-start | bytes 393224 | tf_op jit(solution)/shard_map/ppermute | solution.py:17
  11.1 18.2 %collective-permute-start = (f32[64,4,128]{2,0,1:T(8,128)S(1)}, f32[64,4,128]{2,0,1:T(8,128)S(1)}, u32[]{:S(2)}, u32[]{:S(2)}) collective-permute-start(f32[64,4,128]{2,0,1:T(8,128)S(1)} %bitcast.609), channel_id=1, source_target_pairs={{0,1},{1,2},{2,3},{3,4},{4,5},{5,6},{6,7},{7,8},{8,9},{9,10},{10,1... | collective-permute-start | bytes 393224 | tf_op jit(solution)/shard_map/ppermute | solution.py:17
  55.3 13.9 %collective-permute-start.3 = (f32[64,4,128]{2,0,1:T(8,128)}, f32[64,4,128]{2,0,1:T(8,128)S(1)}, u32[]{:S(2)}, u32[]{:S(2)}) collective-permute-start(f32[64,4,128]{2,0,1:T(8,128)} %bitcast.625), channel_id=1, source_target_pairs={{0,127},{1,0},{2,1},{3,2},{4,3},{5,4},{6,5},{7,6},{8,7},{9,8},{10,... | collective-permute-start | bytes 393224 | tf_op jit(solution)/shard_map/ppermute | solution.py:17
  62.5 10.4 %collective-permute-start.2 = (f32[64,4,128]{2,0,1:T(8,128)}, f32[64,4,128]{2,0,1:T(8,128)S(1)}, u32[]{:S(2)}, u32[]{:S(2)}) collective-permute-start(f32[64,4,128]{2,0,1:T(8,128)} %bitcast.612), channel_id=1, source_target_pairs={{0,1},{1,2},{2,3},{3,4},{4,5},{5,6},{6,7},{7,8},{8,9},{9,10},{10,1... | collective-permute-start | bytes 393224 | tf_op jit(solution)/shard_map/ppermute | solution.py:17
  101.3 10.2 %collective-permute-start.4 = (f32[64,4,128]{2,0,1:T(8,128)}, f32[64,4,128]{2,0,1:T(8,128)S(1)}, u32[]{:S(2)}, u32[]{:S(2)}) collective-permute-start(f32[64,4,128]{2,0,1:T(8,128)} %bitcast.613), channel_id=1, source_target_pairs={{0,1},{1,2},{2,3},{3,4},{4,5},{5,6},{6,7},{7,8},{8,9},{9,10},{10,1... | collective-permute-start | bytes 393224 | tf_op jit(solution)/shard_map/ppermute | solution.py:17
  136.1 10.1 %collective-permute-start.7 = (f32[64,4,128]{2,0,1:T(8,128)}, f32[64,4,128]{2,0,1:T(8,128)S(1)}, u32[]{:S(2)}, u32[]{:S(2)}) collective-permute-start(f32[64,4,128]{2,0,1:T(8,128)} %bitcast.627), channel_id=1, source_target_pairs={{0,127},{1,0},{2,1},{3,2},{4,3},{5,4},{6,5},{7,6},{8,7},{9,8},{10,... | collective-permute-start | bytes 393224 | tf_op jit(solution)/shard_map/ppermute | solution.py:17
  139.6 10.2 %collective-permute-start.6 = (f32[64,4,128]{2,0,1:T(8,128)}, f32[64,4,128]{2,0,1:T(8,128)S(1)}, u32[]{:S(2)}, u32[]{:S(2)}) collective-permute-start(f32[64,4,128]{2,0,1:T(8,128)} %bitcast.614), channel_id=1, source_target_pairs={{0,1},{1,2},{2,3},{3,4},{4,5},{5,6},{6,7},{7,8},{8,9},{9,10},{10,1... | collective-permute-start | bytes 393224 | tf_op jit(solution)/shard_map/ppermute | solution.py:17
  253.3 13.8 %collective-permute-start.19 = (f32[64,4,128]{2,0,1:T(8,128)}, f32[64,4,128]{2,0,1:T(8,128)S(1)}, u32[]{:S(2)}, u32[]{:S(2)}) collective-permute-start(f32[64,4,128]{2,0,1:T(8,128)} %bitcast.628), channel_id=1, source_target_pairs={{0,127},{1,0},{2,1},{3,2},{4,3},{5,4},{6,5},{7,6},{8,7},{9,8},{10,... | collective-permute-start | bytes 393224 | tf_op jit(solution)/shard_map/ppermute | solution.py:17
  260.5 10.2 %collective-permute-start.18 = (f32[64,4,128]{2,0,1:T(8,128)}, f32[64,4,128]{2,0,1:T(8,128)S(1)}, u32[]{:S(2)}, u32[]{:S(2)}) collective-permute-start(f32[64,4,128]{2,0,1:T(8,128)} %bitcast.615), channel_id=1, source_target_pairs={{0,1},{1,2},{2,3},{3,4},{4,5},{5,6},{6,7},{7,8},{8,9},{9,10},{10,1... | collective-permute-start | bytes 393224 | tf_op jit(solution)/shard_map/ppermute | solution.py:17
  299.1 10.2 %collective-permute-start.20 = (f32[64,4,128]{2,0,1:T(8,128)}, f32[64,4,128]{2,0,1:T(8,128)S(1)}, u32[]{:S(2)}, u32[]{:S(2)}) collective-permute-start(f32[64,4,128]{2,0,1:T(8,128)} %bitcast.616), channel_id=1, source_target_pairs={{0,1},{1,2},{2,3},{3,4},{4,5},{5,6},{6,7},{7,8},{8,9},{9,10},{10,1... | collective-permute-start | bytes 393224 | tf_op jit(solution)/shard_map/ppermute | solution.py:17
  334.0 10.6 %collective-permute-start.23 = (f32[64,4,128]{2,0,1:T(8,128)}, f32[64,4,128]{2,0,1:T(8,128)S(1)}, u32[]{:S(2)}, u32[]{:S(2)}) collective-permute-start(f32[64,4,128]{2,0,1:T(8,128)} %bitcast.630), channel_id=1, source_target_pairs={{0,127},{1,0},{2,1},{3,2},{4,3},{5,4},{6,5},{7,6},{8,7},{9,8},{10,... | collective-permute-start | bytes 393224 | tf_op jit(solution)/shard_map/ppermute | solution.py:17
  337.5 10.4 %collective-permute-start.22 = (f32[64,4,128]{2,0,1:T(8,128)}, f32[64,4,128]{2,0,1:T(8,128)S(1)}, u32[]{:S(2)}, u32[]{:S(2)}) collective-permute-start(f32[64,4,128]{2,0,1:T(8,128)} %bitcast.617), channel_id=1, source_target_pairs={{0,1},{1,2},{2,3},{3,4},{4,5},{5,6},{6,7},{7,8},{8,9},{9,10},{10,1... | collective-permute-start | bytes 393224 | tf_op jit(solution)/shard_map/ppermute | solution.py:17
  372.9 10.4 %collective-permute-start.25 = (f32[64,4,128]{2,0,1:T(8,128)}, f32[64,4,128]{2,0,1:T(8,128)S(1)}, u32[]{:S(2)}, u32[]{:S(2)}) collective-permute-start(f32[64,4,128]{2,0,1:T(8,128)} %bitcast.631), channel_id=1, source_target_pairs={{0,127},{1,0},{2,1},{3,2},{4,3},{5,4},{6,5},{7,6},{8,7},{9,8},{10,... | collective-permute-start | bytes 393224 | tf_op jit(solution)/shard_map/ppermute | solution.py:17
  376.7 10.2 %collective-permute-start.24 = (f32[64,4,128]{2,0,1:T(8,128)}, f32[64,4,128]{2,0,1:T(8,128)S(1)}, u32[]{:S(2)}, u32[]{:S(2)}) collective-permute-start(f32[64,4,128]{2,0,1:T(8,128)} %bitcast.618), channel_id=1, source_target_pairs={{0,1},{1,2},{2,3},{3,4},{4,5},{5,6},{6,7},{7,8},{8,9},{9,10},{10,1... | collective-permute-start | bytes 393224 | tf_op jit(solution)/shard_map/ppermute | solution.py:17
  411.7 10.5 %collective-permute-start.27 = (f32[64,4,128]{2,0,1:T(8,128)}, f32[64,4,128]{2,0,1:T(8,128)S(1)}, u32[]{:S(2)}, u32[]{:S(2)}) collective-permute-start(f32[64,4,128]{2,0,1:T(8,128)} %bitcast.632), channel_id=1, source_target_pairs={{0,127},{1,0},{2,1},{3,2},{4,3},{5,4},{6,5},{7,6},{8,7},{9,8},{10,... | collective-permute-start | bytes 393224 | tf_op jit(solution)/shard_map/ppermute | solution.py:17
  415.2 10.2 %collective-permute-start.26 = (f32[64,4,128]{2,0,1:T(8,128)}, f32[64,4,128]{2,0,1:T(8,128)S(1)}, u32[]{:S(2)}, u32[]{:S(2)}) collective-permute-start(f32[64,4,128]{2,0,1:T(8,128)} %bitcast.619), channel_id=1, source_target_pairs={{0,1},{1,2},{2,3},{3,4},{4,5},{5,6},{6,7},{7,8},{8,9},{9,10},{10,1... | collective-permute-start | bytes 393224 | tf_op jit(solution)/shard_map/ppermute | solution.py:17
  450.4 10.6 %collective-permute-start.29 = (f32[64,4,128]{2,0,1:T(8,128)}, f32[64,4,128]{2,0,1:T(8,128)S(1)}, u32[]{:S(2)}, u32[]{:S(2)}) collective-permute-start(f32[64,4,128]{2,0,1:T(8,128)} %bitcast.633), channel_id=1, source_target_pairs={{0,127},{1,0},{2,1},{3,2},{4,3},{5,4},{6,5},{7,6},{8,7},{9,8},{10,... | collective-permute-start | bytes 393224 | tf_op jit(solution)/shard_map/ppermute | solution.py:17
  454.2 10.4 %collective-permute-start.28 = (f32[64,4,128]{2,0,1:T(8,128)}, f32[64,4,128]{2,0,1:T(8,128)S(1)}, u32[]{:S(2)}, u32[]{:S(2)}) collective-permute-start(f32[64,4,128]{2,0,1:T(8,128)} %bitcast.620), channel_id=1, source_target_pairs={{0,1},{1,2},{2,3},{3,4},{4,5},{5,6},{6,7},{7,8},{8,9},{9,10},{10,1... | collective-permute-start | bytes 393224 | tf_op jit(solution)/shard_map/ppermute | solution.py:17
  492.7 10.2 %collective-permute-start.30 = (f32[64,4,128]{2,0,1:T(8,128)}, f32[64,4,128]{2,0,1:T(8,128)S(1)}, u32[]{:S(2)}, u32[]{:S(2)}) collective-permute-start(f32[64,4,128]{2,0,1:T(8,128)} %bitcast.610), channel_id=1, source_target_pairs={{0,1},{1,2},{2,3},{3,4},{4,5},{5,6},{6,7},{7,8},{8,9},{9,10},{10,1... | collective-permute-start | bytes 393224 | tf_op jit(solution)/shard_map/ppermute | solution.py:17
  606.2 13.9 %collective-permute-start.41 = (f32[64,4,128]{2,0,1:T(8,128)}, f32[64,4,128]{2,0,1:T(8,128)S(1)}, u32[]{:S(2)}, u32[]{:S(2)}) collective-permute-start(f32[64,4,128]{2,0,1:T(8,128)} %bitcast.634), channel_id=1, source_target_pairs={{0,127},{1,0},{2,1},{3,2},{4,3},{5,4},{6,5},{7,6},{8,7},{9,8},{10,... | collective-permute-start | bytes 393224 | tf_op jit(solution)/shard_map/ppermute | solution.py:17
  613.4 10.4 %collective-permute-start.40 = (f32[64,4,128]{2,0,1:T(8,128)}, f32[64,4,128]{2,0,1:T(8,128)S(1)}, u32[]{:S(2)}, u32[]{:S(2)}) collective-permute-start(f32[64,4,128]{2,0,1:T(8,128)} %bitcast.621), channel_id=1, source_target_pairs={{0,1},{1,2},{2,3},{3,4},{4,5},{5,6},{6,7},{7,8},{8,9},{9,10},{10,1... | collective-permute-start | bytes 393224 | tf_op jit(solution)/shard_map/ppermute | solution.py:17
  685.8 10.8 %collective-permute-start.45 = (f32[64,4,128]{2,0,1:T(8,128)}, f32[64,4,128]{2,0,1:T(8,128)S(1)}, u32[]{:S(2)}, u32[]{:S(2)}) collective-permute-start(f32[64,4,128]{2,0,1:T(8,128)} %bitcast.623), channel_id=1, source_target_pairs={{0,127},{1,0},{2,1},{3,2},{4,3},{5,4},{6,5},{7,6},{8,7},{9,8},{10,... | collective-permute-start | bytes 393224 | tf_op jit(solution)/shard_map/ppermute | solution.py:17
  (72 other events, 640.9 us)
where the time goes:
time: 723 us; the launch traced here: 716 us
  matrix products  285 us (39%)
  local copies, waits for them, and re-layouts  143 us (20%)
  starting transfers between devices  129 us (18%)
  blocking collectives  72.2 us (10%)
  waiting for transfers between devices  56.4 us (8%)
  other arithmetic  29.5 us (4%)
    dot_general x14, matrix products, fine_op(): jnp.einsum('ikab,rikb->ria', off_blocks, picked, precision=hp)  180 us
    ppermute x46, starting transfers between devices, from_behind(): return lax.ppermute(value, axis, pairs)  129 us
    dot_general x14, matrix products, fine_op(): result = jnp.einsum('iab,rib->ria', diag_blocks, blocks_view, precision=hp)  89.4 us
    all_gather x2, blocking collectives, local(): gathered = lax.all_gather(coarse_resid_two, 'dom', axis=1, tiled=True)  72.2 us
    ppermute x46, waiting for transfers between devices, from_behind(): return lax.ppermute(value, axis, pairs)  56.4 us
    gather x14, local copies, waits for them, and re-layouts, fine_op(): picked = extended[:, block_cols, :]  50.3 us
    gather x14, local copies, waits for them, and re-layouts, fine_op(): to_lower = blocks_view[:, lists[0], :]  31.9 us
    gather x14, local copies, waits for them, and re-layouts, fine_op(): to_upper = blocks_view[:, lists[1], :]  30.9 us
  transfers between devices with their start and end apart: 46, of which 29 were waited for; matrix products, arithmetic and copies ran while one was open for 15% of the time, Pallas kernels for 0%

commit v1 on v0

v1 whole, which is shorter than its diff:
```python
import jax
import jax.numpy as jnp
from jax import lax
from jax.experimental import pallas as pl
from jax.experimental.pallas import tpu as pltpu
from jax.sharding import PartitionSpec as P

MESH = pl.DeviceIdType.MESH
RELAX = 0.6
SMOOTH = 0.5
F32 = jnp.float32
BF16 = jnp.bfloat16
CHUNK = 4


def split(x):
    hi = x.astype(BF16)
    lo = (x - hi.astype(F32)).astype(BF16)
    return jnp.concatenate([hi, lo], axis=0)


def split_columns(x):
    hi = x.astype(BF16)
    lo = (x - hi.astype(F32)).astype(BF16)
    return jnp.concatenate([hi, lo], axis=1)


def fold(res, rows, width):
    return res[:rows, :width] + res[:rows, width:] + res[rows:, :width]


def kernel(
    cols_in, lists_in,
    rhs_hbm, diag_hbm, off_hbm, agg_ref, cdiag_ref, cside_ref, cagg_ref, inv_hbm,
    out_ref,
    perm, pos, cols, sent_pos,
    rhs_v, diag_v, off_v, inv_v, weights, xs, x_ref, r_ref, u_ref, f_ref, dnat, dinv, table, tbuf,
    first8, send, recv, cw, cx, csend, crecv, inv_s, gtile, gather, gfull,
    load_sem, off_sem, send_sem, recv_sem, csend_sem, crecv_sem, gsend_sem, grecv_sem,
):
    nright, nrows, width = f_ref.shape[1], f_ref.shape[0], f_ref.shape[2]
    me = lax.axis_index("dom")
    count = 128
    upper = lax.rem(me + 1, count)
    lower = lax.rem(me + count - 1, count)
    core = lax.rem(me, 2)
    y = lax.rem(me // 2, 4)
    z = lax.rem(me // 8, 4)
    xc = me // 32
    partner = me + 1 - 2 * core

    def member(ax, step):
        if ax == 0:
            return me + 2 * (lax.rem(y + step, 4) - y)
        if ax == 1:
            return me + 8 * (lax.rem(z + step, 4) - z)
        return me + 32 * (lax.rem(xc + step, 4) - xc)

    load_rhs = pltpu.make_async_copy(rhs_hbm, rhs_v, load_sem.at[0])
    load_diag = pltpu.make_async_copy(diag_hbm, diag_v, load_sem.at[1])
    load_inv = pltpu.make_async_copy(
        inv_hbm.at[pl.ds(pl.multiple_of(me * 8, 8), 8)], inv_v, load_sem.at[2]
    )
    load_diag.start()
    load_rhs.start()

    def load_off(c):
        rows = pl.ds(c * CHUNK, CHUNK)
        return pltpu.make_async_copy(off_hbm.at[rows], off_v.at[rows], off_sem.at[c])

    for c in range(nrows // CHUNK):
        load_off(c).start()
    load_inv.start()

    barrier = pltpu.get_barrier_semaphore()
    peers = [upper, lower] + [member(ax, s) for ax in range(3) for s in (1, 2, 3)]
    for peer in peers:
        pl.semaphore_signal(barrier, inc=1, device_id=(peer,), device_id_type=MESH)

    wanted = [lists_in[m] for m in range(8)]

    def count_sent(i, total):
        flag = wanted[0] == i
        for m in range(1, 8):
            flag = jnp.logical_or(flag, wanted[m] == i)
        value = flag.astype(jnp.int32)
        pos[i] = value
        return total + value

    nsent = lax.fori_loop(0, nrows, count_sent, jnp.int32(0))

    def place(i, carry):
        a, b = carry
        value = pos[i]
        pos[i] = jnp.where(value == 1, a, b)
        return a + value, b + 1 - value

    lax.fori_loop(0, nrows, place, (jnp.int32(0), nsent))

    def invert(j, _):
        total = jnp.int32(0)
        for i in range(nrows):
            total = total + jnp.where(pos[i] == j, i, 0)
        perm[j] = total
        for k in range(3):
            c = cols_in[total * 3 + k]
            own = pos[jnp.minimum(c, nrows - 1)]
            cols[j * 3 + k] = jnp.where(c < nrows, own, c)
        return 0

    lax.fori_loop(0, nrows, invert, 0)
    for m in range(8):
        sent_pos[m] = pos[wanted[m]]

    def halo_copies(n):
        slot = lax.rem(n, 3)
        up = pltpu.make_async_remote_copy(
            src_ref=send.at[slot, 1], dst_ref=recv.at[slot, 0],
            send_sem=send_sem.at[slot, 1], recv_sem=recv_sem.at[slot, 0],
            device_id=(upper,), device_id_type=MESH,
        )
        down = pltpu.make_async_remote_copy(
            src_ref=send.at[slot, 0], dst_ref=recv.at[slot, 1],
            send_sem=send_sem.at[slot, 0], recv_sem=recv_sem.at[slot, 1],
            device_id=(lower,), device_id_type=MESH,
        )
        return up, down

    def halo_send(n):
        slot = lax.rem(n, 3)
        for m in range(8):
            send[slot, m // 4, m % 4] = first8[sent_pos[m]]
        up, down = halo_copies(n)
        up.start()
        down.start()

    def halo_sent(n):
        for copy in halo_copies(n):
            copy.wait_send()

    def halo_take(n):
        slot, par = lax.rem(n, 3), lax.rem(n, 2)
        for copy in halo_copies(n):
            copy.wait_recv()
        for m in range(8):
            xs[par, nrows + m] = split(recv[slot, m // 4, m % 4])

    def product(par, j):
        parts = [xs[par, j]] + [xs[par, cols[j * 3 + k]] for k in range(3)]
        res = jnp.dot(
            jnp.concatenate(parts, axis=1), weights[perm[j]], preferred_element_type=F32
        )
        return fold(res, nright, width)

    def rows_first(body):
        for j in range(8):
            body(j, j)

    def rows_rest(body):
        def step(g, _):
            for u in range(8):
                body(8 + g * 8 + u, None)
            return 0

        lax.fori_loop(0, (nrows - 8) // 8, step, 0)

    def publish(par, j, fixed, v):
        xs[1 - par, j] = split(v)
        if fixed is not None:
            first8[fixed] = v

    rows_iota = lax.broadcasted_iota(jnp.int32, (width, width), 0)
    eye = rows_iota == lax.broadcasted_iota(jnp.int32, (width, width), 1)
    load_diag.wait()

    def take_diag(i, _):
        d = jnp.sum(jnp.where(eye, diag_v[i], 0.0), axis=0, keepdims=True)
        dnat[i] = 1.0 / d
        return 0

    lax.fori_loop(0, nrows, take_diag, 0)
    load_rhs.wait()
    for i in range(nrows):
        u_ref[i] = rhs_v[:, i * width:(i + 1) * width]

    def start_row(j, fixed):
        d = dnat[perm[j]]
        dinv[j] = d
        f = u_ref[perm[j]]
        f_ref[j] = f
        v = RELAX * d * f
        x_ref[j] = v
        publish(jnp.int32(1), j, fixed, v)

    rows_first(start_row)
    pl.semaphore_wait(barrier, len(peers))
    halo_send(jnp.int32(0))
    rows_rest(start_row)

    def convert(c, _):
        load_off(c).wait()
        for q in range(CHUNK):
            i = c * CHUNK + q
            weights[i, 0:width] = split_columns(diag_v[i].T)
            for k in range(3):
                weights[i, (k + 1) * width:(k + 2) * width] = split_columns(off_v[i, k].T)
        return 0

    lax.fori_loop(0, nrows // CHUNK, convert, 0)

    def make_table(j, sums):
        hot = (agg_ref[perm[j]] == rows_iota).astype(F32)
        table[j] = hot.astype(BF16)
        return sums + hot

    sums = lax.fori_loop(0, nrows, make_table, jnp.zeros((width, width), F32))
    count_one = jnp.sum(sums, axis=1, keepdims=True)
    scale_one = (1.0 / jnp.sqrt(jnp.broadcast_to(count_one, (width, width)))).T[0:1]
    hot_two = (cagg_ref[...] == lax.broadcasted_iota(jnp.int32, (8, width), 0)).astype(F32)
    table_two = hot_two * (1.0 / jnp.sqrt(jnp.sum(hot_two, axis=1, keepdims=True)))
    table_two_pad = jnp.concatenate([table_two, jnp.zeros((width - 8, width), F32)], axis=0)
    cd = cdiag_ref[0]
    d1inv = 1.0 / jnp.sum(jnp.where(eye, cd, 0.0), axis=0, keepdims=True)
    cw[0:width] = split_columns(cd.T)
    cw[width:2 * width] = split_columns(cside_ref[0, 0].T)
    cw[2 * width:3 * width] = split_columns(cside_ref[0, 1].T)
    load_inv.wait()
    inv_s[...] = split(inv_v[...])

    def coarse_copies(m):
        slot = lax.rem(m, 3)
        up = pltpu.make_async_remote_copy(
            src_ref=csend.at[slot], dst_ref=crecv.at[slot, 0],
            send_sem=csend_sem.at[slot, 1], recv_sem=crecv_sem.at[slot, 0],
            device_id=(upper,), device_id_type=MESH,
        )
        down = pltpu.make_async_remote_copy(
            src_ref=csend.at[slot], dst_ref=crecv.at[slot, 1],
            send_sem=csend_sem.at[slot, 0], recv_sem=crecv_sem.at[slot, 1],
            device_id=(lower,), device_id_type=MESH,
        )
        return up, down

    def coarse_op(value, m):
        slot = lax.rem(m, 3)
        csend[slot] = value
        copies = coarse_copies(m)
        for copy in copies:
            copy.start()
        for copy in copies:
            copy.wait()
        lhs = jnp.concatenate(
            [split(value), split(crecv[slot, 0]), split(crecv[slot, 1])], axis=1
        )
        return fold(jnp.dot(lhs, cw[...], preferred_element_type=F32), nright, width)

    chip = me // 2

    def gather_copies(cyc, ax):
        size = (1, 4, 16)[ax]
        first = (chip // size) * size
        out = []
        for s in (1, 2, 3):
            where = gather.at[cyc, pl.ds(first, size)]
            out.append(pltpu.make_async_remote_copy(
                src_ref=where, dst_ref=where,
                send_sem=gsend_sem.at[cyc, ax * 3 + s], recv_sem=grecv_sem.at[cyc, ax * 3 + s],
                device_id=(member(ax, s),), device_id_type=MESH,
            ))
        return out

    def gather_waits(cyc, ax):
        size = (1, 4, 16)[ax]
        for s in (1, 2, 3):
            source = member(ax, 4 - s) // 2
            where = gather.at[cyc, pl.ds((source // size) * size, size)]
            pltpu.make_async_remote_copy(
                src_ref=where, dst_ref=where,
                send_sem=gsend_sem.at[cyc, ax * 3 + s], recv_sem=grecv_sem.at[cyc, ax * 3 + s],
                device_id=(member(ax, s),), device_id_type=MESH,
            ).wait_recv()

    def gather_all(cyc, tile):
        gtile[cyc, 0] = tile
        pair = pltpu.make_async_remote_copy(
            src_ref=gtile.at[cyc, 0], dst_ref=gtile.at[cyc, 1],
            send_sem=gsend_sem.at[cyc, 0], recv_sem=grecv_sem.at[cyc, 0],
            device_id=(partner,), device_id_type=MESH,
        )
        pair.start()
        pair.wait()
        other = gtile[cyc, 1]
        even = jnp.where(core == 0, tile, other)
        odd = jnp.where(core == 0, other, tile)
        low_lanes = lax.broadcasted_iota(jnp.int32, (8, width), 1) < nright
        gather[cyc, pl.ds(chip, 1)] = jnp.where(low_lanes, even, pltpu.roll(odd, nright, 1))[None]
        for ax in range(3):
            copies = gather_copies(cyc, ax)
            for copy in copies:
                copy.start()
            gather_waits(cyc, ax)
            for copy in copies:
                copy.wait_send()
        for c in range(64):
            pair_tile = gather[cyc, c]
            gfull[16 * c:16 * c + 8] = split_columns(pair_tile)
            gfull[16 * c + 8:16 * c + 16] = split_columns(pltpu.roll(pair_tile, nright, 1))

    def sweep(n, last):
        par = lax.rem(n, 2)
        halo_take(n)

        def body(j, fixed):
            d = RELAX * dinv[j]
            new = x_ref[j] + d * (f_ref[j] - product(par, j))
            x_ref[j] = new
            publish(par, j, fixed, new)

        rows_first(body)
        if last is None:
            halo_send(n + 1)
        else:
            @pl.when(n < last)
            def _():
                halo_send(n + 1)
        rows_rest(body)
        if last is None:
            halo_sent(n + 1)
        else:
            @pl.when(n < last)
            def _():
                halo_sent(n + 1)

    halo_sent(jnp.int32(0))
    sweep(jnp.int32(0), None)

    def cycle(cyc, _):
        n = 1 + 7 * cyc
        par = lax.rem(n, 2)
        halo_take(n)

        def resid_row(j, fixed):
            r = f_ref[j] - product(par, j)
            r_ref[j] = r
            publish(par, j, fixed, dinv[j] * r)

        rows_first(resid_row)
        halo_send(n + 1)
        rows_rest(resid_row)
        halo_sent(n + 1)

        n1 = n + 1
        par1 = lax.rem(n1, 2)
        halo_take(n1)

        def smooth_row(j, fixed):
            tbuf[j] = split(r_ref[j] - SMOOTH * product(par1, j))

        rows_first(smooth_row)
        rows_rest(smooth_row)

        def restrict(g, acc):
            for u in range(8):
                j = g * 8 + u
                acc = acc + lax.dot_general(
                    tbuf[j], table[j], (((1,), (1,)), ((), ())), preferred_element_type=F32
                )
            return acc

        acc = lax.fori_loop(0, nrows // 8, restrict, jnp.zeros((2 * nright, width), F32))
        right_one = (acc[:nright] + acc[nright:]) * scale_one

        m = 4 * cyc
        it = RELAX * d1inv * right_one
        it = it + RELAX * d1inv * (right_one - coarse_op(it, m))
        resid_one = right_one - coarse_op(it, m + 1)
        padded = jnp.concatenate([resid_one, jnp.zeros((width - nright, width), F32)], axis=0)
        tile = lax.dot_general(
            table_two, padded, (((1,), (1,)), ((), ())),
            precision=lax.Precision.HIGHEST, preferred_element_type=F32,
        )
        gather_all(cyc, tile)
        e2 = fold(jnp.dot(inv_s[...], gfull[...], preferred_element_type=F32), 8, width)
        e2t = jnp.concatenate([e2, jnp.zeros((width - 8, width), F32)], axis=0).T[:nright]
        it = it + jnp.dot(
            e2t, table_two_pad, precision=lax.Precision.HIGHEST, preferred_element_type=F32
        )
        it = it + RELAX * d1inv * (right_one - coarse_op(it, m + 2))
        it = it + RELAX * d1inv * (right_one - coarse_op(it, m + 3))
        cx[...] = split(it * scale_one)

        n2 = n + 2
        par2 = lax.rem(n2, 2)

        def lift_row(j, fixed):
            res = jnp.dot(cx[...], table[j], preferred_element_type=F32)
            u = res[:nright] + res[nright:]
            u_ref[j] = u
            publish(1 - par2, j, fixed, u)

        rows_first(lift_row)
        halo_send(n2)
        rows_rest(lift_row)
        halo_sent(n2)
        halo_take(n2)

        def correct_row(j, fixed):
            d = SMOOTH * dinv[j]
            new = x_ref[j] + u_ref[j] - d * product(par2, j)
            x_ref[j] = new
            publish(par2, j, fixed, new)

        rows_first(correct_row)
        halo_send(n2 + 1)
        rows_rest(correct_row)
        halo_sent(n2 + 1)

        def sweeps(s, _):
            sweep(n2 + 1 + s, 12)
            return 0

        lax.fori_loop(0, 4 - 2 * cyc, sweeps, 0)
        return 0

    lax.fori_loop(0, 2, cycle, 0)
    for i in range(nrows):
        out_ref[:, i * width:(i + 1) * width] = x_ref[pos[i]]


def local(
    rhs_fields, diag_blocks, off_blocks, block_cols, send_lists, fine_agg,
    coarse_diag, coarse_side, coarse_agg, coarse_inverse,
):
    nrows, width = diag_blocks.shape[0], diag_blocks.shape[1]
    nright = rhs_fields.shape[0]
    naggs = coarse_diag.shape[1]
    S = pl.BlockSpec(memory_space=pltpu.SMEM)
    V = pl.BlockSpec(memory_space=pltpu.VMEM)
    A = pl.BlockSpec(memory_space=pl.ANY)
    DMA = pltpu.SemaphoreType.DMA
    return pl.pallas_call(
        kernel,
        name="multigrid",
        out_shape=jax.ShapeDtypeStruct(rhs_fields.shape, F32),
        in_specs=[S, S, A, A, A, V, V, V, V, A],
        out_specs=V,
        scratch_shapes=[
            pltpu.SMEM((nrows,), jnp.int32),
            pltpu.SMEM((nrows,), jnp.int32),
            pltpu.SMEM((3 * nrows,), jnp.int32),
            pltpu.SMEM((8,), jnp.int32),
            pltpu.VMEM(rhs_fields.shape, F32),
            pltpu.VMEM(diag_blocks.shape, F32),
            pltpu.VMEM(off_blocks.shape, F32),
            pltpu.VMEM((8, coarse_inverse.shape[1]), F32),
            pltpu.VMEM((nrows, 4 * width, 2 * width), BF16),
            pltpu.VMEM((2, nrows + 8, 2 * nright, width), BF16),
            pltpu.VMEM((nrows, nright, width), F32),
            pltpu.VMEM((nrows, nright, width), F32),
            pltpu.VMEM((nrows, nright, width), F32),
            pltpu.VMEM((nrows, nright, width), F32),
            pltpu.VMEM((nrows, 1, width), F32),
            pltpu.VMEM((nrows, 1, width), F32),
            pltpu.VMEM((nrows, naggs, width), BF16),
            pltpu.VMEM((nrows, 2 * nright, width), BF16),
            pltpu.VMEM((8, nright, width), F32),
            pltpu.VMEM((3, 2, 4, nright, width), F32),
            pltpu.VMEM((3, 2, 4, nright, width), F32),
            pltpu.VMEM((3 * width, 2 * width), BF16),
            pltpu.VMEM((2 * nright, width), BF16),
            pltpu.VMEM((3, nright, width), F32),
            pltpu.VMEM((3, 2, nright, width), F32),
            pltpu.VMEM((16, coarse_inverse.shape[1]), BF16),
            pltpu.VMEM((2, 2, 8, width), F32),
            pltpu.VMEM((2, 64, 8, width), F32),
            pltpu.VMEM((1024, 2 * width), BF16),
            DMA((3,)),
            DMA((nrows // CHUNK,)),
            DMA((3, 2)),
            DMA((3, 2)),
            DMA((3, 2)),
            DMA((3, 2)),
            DMA((2, 10)),
            DMA((2, 10)),
        ],
        compiler_params=pltpu.CompilerParams(
            collective_id=0, has_side_effects=True, vmem_limit_bytes=60 * 1024 * 1024
        ),
    )(
        block_cols.reshape(-1), send_lists.reshape(-1),
        rhs_fields, diag_blocks, off_blocks, fine_agg.reshape(nrows, 1, width),
        coarse_diag, coarse_side, coarse_agg.reshape(1, naggs), coarse_inverse,
    )


def solution(mesh):
    return jax.shard_map(
        local,
        mesh=mesh,
        in_specs=(
            P(None, "dom"),
            P("dom", None, None),
            P("dom", None, None, None),
            P("dom", None),
            P("dom", None, None),
            P("dom"),
            P("dom", None, None),
            P("dom", None, None, None),
            P("dom"),
            P(),
        ),
        out_specs=P(None, "dom"),
        check_vma=False,
    )
```

time: 723 us -> 192 us (0.27)
  matrix products: 285 us -> 0 us
  Pallas kernels: 0 us -> 187 us
  local copies, waits for them, and re-layouts: 143 us -> 5 us
  starting transfers between devices: 129 us -> 0 us
  blocking collectives: 72.2 us -> 0 us
  waiting for transfers between devices: 56.4 us -> 0 us
  other arithmetic: 29.5 us -> 0 us
    dot_general x65 -> x0, matrix products: 285 us -> none  [the longest x14 180 us: fine_op(): jnp.einsum('ikab,rikb->ria', off_blocks, picked, precision=hp)]
    pallas_call x0 -> x1, Pallas kernels: none -> 187 us  [local(): pl.pallas_call(kernel, name='multigrid', out_shape=jax.ShapeDtypeStruct(r...]
    ppermute x46 -> x0, starting transfers between devices: 129 us -> none  [from_behind(): return lax.ppermute(value, axis, pairs)]
    gather x44 -> x0, local copies, waits for them, and re-layouts: 116 us -> none  [the longest x14 50.3 us: fine_op(): picked = extended[:, block_cols, :]]
    all_gather x2 -> x0, blocking collectives: 72.2 us -> none  [local(): gathered = lax.all_gather(coarse_resid_two, 'dom', axis=1, tiled=True)]
    ppermute x46 -> x0, waiting for transfers between devices: 56.4 us -> none  [from_behind(): return lax.ppermute(value, axis, pairs)]
    concatenate x15 -> x0, other arithmetic: 17 us -> none  [the longest x14 17 us: fine_op(): extended = jnp.concatenate([blocks_view, from_lower, from_upper], axis=1)]
    unnamed x101 -> x2, local copies, waits for them, and re-layouts: 19.2 us -> 3.03 us
  transfers between devices with their start and end apart: 46 -> 0, of which waited for: 29 -> 0; matrix products, arithmetic and copies ran while one was open for 15% -> 0% of each run, Pallas kernels for 0% -> 0%
where the time goes in v1:
time: 192 us
  Pallas kernels  187 us (97%)
  local copies, waits for them, and re-layouts  5 us (3%)
    pallas_call x1, Pallas kernels, local(): pl.pallas_call(kernel, name='multigrid', out_shape=jax.ShapeDtypeStruct(r...  187 us

profile of v1, /device:TPU:0, one launch (start us, length us, event | category | flops | bytes accessed | tf_op | source)
XLA Modules:
  0.0 192.1 jit_solution(8860137396480944100)
XLA Ops:
  0.0 1.3 reshape.13.lists_in
  1.3 0.8 copy.12
  2.1 0.6 reshape.12.cols_in
  2.7 187.1 %multigrid.1 = f32[64,4096]{1,0:T(8,128)} custom-call(s32[96]{0:T(128)} %reshape.12.cols_in, s32[8]{0:T(128)} %reshape.13.lists_in, f32[64,4096]{1,0:T(8,128)} %rhs_hbm.1, f32[32,128,128]{2,1,0:T(8,128)} %diag_hbm.1, f32[32,3,128,128]{3,2,1,0:T(8,128)} %off_hbm.1, s32[32,1,128]{2,1,0:T(1,128)} %bitcast.2, f32[1,128,128]{2,1,0:T(8,128)} %cdiag_ref.1, ...), custom_call_target="tpu_custom_call" | custom-call | tf_op jit(solution)/shard_map/multigrid/pallas_call | solution.py:441
  189.8 2.3 %copy.14 = f32[64,4096]{1,0:T(8,128)} copy(f32[64,4096]{1,0:T(8,128)} %multigrid.1) | data formatting | bytes 2097152

commit v2 on v1

--- a/solution.py
+++ b/solution.py
@@ -11,6 +11,7 @@
 F32 = jnp.float32
 BF16 = jnp.bfloat16
 CHUNK = 4
+OFFSETS = (1, -1, 2, -2, 3, -3, 4, -4)
 
 
 def split(x):
@@ -35,8 +36,10 @@
     out_ref,
     perm, pos, cols, sent_pos,
     rhs_v, diag_v, off_v, inv_v, weights, xs, x_ref, r_ref, u_ref, f_ref, dnat, dinv, table, tbuf,
-    first8, send, recv, cw, cx, csend, crecv, inv_s, gtile, gather, gfull,
-    load_sem, off_sem, send_sem, recv_sem, csend_sem, crecv_sem, gsend_sem, grecv_sem,
+    first8, send, recv, cw, cx, small, big_diag, big_side, fbuf, tw, near_table, inv_s,
+    gtile, gather, gfull,
+    load_sem, off_sem, send_sem, recv_sem, small_send, small_recv, big_send, big_recv,
+    fsend_sem, frecv_sem, gsend_sem, grecv_sem,
 ):
     nright, nrows, width = f_ref.shape[1], f_ref.shape[0], f_ref.shape[2]
     me = lax.axis_index("dom")
@@ -58,9 +61,16 @@
 
     load_rhs = pltpu.make_async_copy(rhs_hbm, rhs_v, load_sem.at[0])
     load_diag = pltpu.make_async_copy(diag_hbm, diag_v, load_sem.at[1])
-    load_inv = pltpu.make_async_copy(
-        inv_hbm.at[pl.ds(pl.multiple_of(me * 8, 8), 8)], inv_v, load_sem.at[2]
-    )
+    def at_offset(o):
+        return lax.rem(me + o + count, count)
+
+    load_inv = [
+        pltpu.make_async_copy(
+            inv_hbm.at[pl.ds(pl.multiple_of(at_offset(o) * 8, 8), 8)],
+            inv_v.at[o + 3], load_sem.at[5 + o],
+        )
+        for o in range(-3, 4)
+    ]
     load_diag.start()
     load_rhs.start()
 
@@ -70,10 +80,11 @@
 
     for c in range(nrows // CHUNK):
         load_off(c).start()
-    load_inv.start()
+    for load in load_inv:
+        load.start()
 
     barrier = pltpu.get_barrier_semaphore()
-    peers = [upper, lower] + [member(ax, s) for ax in range(3) for s in (1, 2, 3)]
+    peers = [at_offset(o) for o in OFFSETS] + [member(ax, s) for ax in range(3) for s in (1, 2, 3)]
     for peer in peers:
         pl.semaphore_signal(barrier, inc=1, device_id=(peer,), device_id_type=MESH)
 
@@ -197,6 +208,22 @@
     halo_send(jnp.int32(0))
     rows_rest(start_row)
 
+    def big_copies(o):
+        return [
+            pltpu.make_async_remote_copy(
+                src_ref=src, dst_ref=dst.at[3 - o],
+                send_sem=big_send.at[i, 3 - o], recv_sem=big_recv.at[i, 3 - o],
+                device_id=(at_offset(o),), device_id_type=MESH,
+            )
+            for i, (src, dst) in enumerate(
+                [(cdiag_ref.at[0], big_diag), (cside_ref.at[0], big_side)]
+            )
+        ]
+
+    for o in OFFSETS[:6]:
+        for copy in big_copies(o):
+            copy.start()
+
     def convert(c, _):
         load_off(c).wait()
         for q in range(CHUNK):
@@ -218,41 +245,63 @@
     scale_one = (1.0 / jnp.sqrt(jnp.broadcast_to(count_one, (width, width)))).T[0:1]
     hot_two = (cagg_ref[...] == lax.broadcasted_iota(jnp.int32, (8, width), 0)).astype(F32)
     table_two = hot_two * (1.0 / jnp.sqrt(jnp.sum(hot_two, axis=1, keepdims=True)))
-    table_two_pad = jnp.concatenate([table_two, jnp.zeros((width - 8, width), F32)], axis=0)
     cd = cdiag_ref[0]
     d1inv = 1.0 / jnp.sum(jnp.where(eye, cd, 0.0), axis=0, keepdims=True)
-    cw[0:width] = split_columns(cd.T)
-    cw[width:2 * width] = split_columns(cside_ref[0, 0].T)
-    cw[2 * width:3 * width] = split_columns(cside_ref[0, 1].T)
-    load_inv.wait()
-    inv_s[...] = split(inv_v[...])
-
-    def coarse_copies(m):
-        slot = lax.rem(m, 3)
-        up = pltpu.make_async_remote_copy(
-            src_ref=csend.at[slot], dst_ref=crecv.at[slot, 0],
-            send_sem=csend_sem.at[slot, 1], recv_sem=crecv_sem.at[slot, 0],
-            device_id=(upper,), device_id_type=MESH,
-        )
-        down = pltpu.make_async_remote_copy(
-            src_ref=csend.at[slot], dst_ref=crecv.at[slot, 1],
-            send_sem=csend_sem.at[slot, 0], recv_sem=crecv_sem.at[slot, 1],
-            device_id=(lower,), device_id_type=MESH,
-        )
-        return up, down
-
-    def coarse_op(value, m):
-        slot = lax.rem(m, 3)
-        csend[slot] = value
-        copies = coarse_copies(m)
-        for copy in copies:
-            copy.start()
-        for copy in copies:
-            copy.wait()
-        lhs = jnp.concatenate(
-            [split(value), split(crecv[slot, 0]), split(crecv[slot, 1])], axis=1
-        )
-        return fold(jnp.dot(lhs, cw[...], preferred_element_type=F32), nright, width)
+    lists = [agg_ref[wanted[m]].astype(F32) for m in range(8)]
+    small[4] = jnp.concatenate(
+        [d1inv, scale_one, cagg_ref[...].astype(F32), jnp.zeros((1, width), F32)]
+        + lists + [jnp.zeros((4, width), F32)],
+        axis=0,
+    )
+
+    def small_copy(o):
+        return pltpu.make_async_remote_copy(
+            src_ref=small.at[4], dst_ref=small.at[4 - o],
+            send_sem=small_send.at[4 - o], recv_sem=small_recv.at[4 - o],
+            device_id=(at_offset(o),), device_id_type=MESH,
+        )
+
+    for o in OFFSETS:
+        small_copy(o).start()
+    big_diag[3] = cd
+    big_side[3] = cside_ref[0]
+    for load in load_inv:
+        load.wait()
+    inv_s[...] = split(jnp.concatenate([inv_v[k] for k in range(7)], axis=0))
+    float_rows = rows_iota.astype(F32)
+
+    def take_near():
+        for o in OFFSETS[:6]:
+            for copy in big_copies(o):
+                copy.wait()
+        for o in OFFSETS:
+            small_copy(o).wait()
+
+        def weigh(k, _):
+            cw[k, 0:width] = split_columns(big_diag[k].T)
+            cw[k, width:2 * width] = split_columns(big_side[k, 0].T)
+            cw[k, 2 * width:3 * width] = split_columns(big_side[k, 1].T)
+            shift = (8 * k).astype(F32)
+            hot = ((small[k + 1, 2:3] + shift) == float_rows).astype(F32)
+            members = jnp.maximum(jnp.sum(hot, axis=1, keepdims=True), 1.0)
+            tw[k] = split_columns(hot * (1.0 / jnp.sqrt(members)))
+            return 0
+
+        lax.fori_loop(0, 7, weigh, 0)
+        for m in range(4):
+            near_table[m] = (small[3, 8 + m:9 + m] == float_rows).astype(BF16)
+            near_table[4 + m] = (small[5, 4 + m:5 + m] == float_rows).astype(BF16)
+
+    def coarse_copy(cyc, o):
+        return pltpu.make_async_remote_copy(
+            src_ref=fbuf.at[cyc, 4], dst_ref=fbuf.at[cyc, 4 - o],
+            send_sem=fsend_sem.at[cyc, 4 - o], recv_sem=frecv_sem.at[cyc, 4 - o],
+            device_id=(at_offset(o),), device_id_type=MESH,
+        )
+
+    def coarse_op(o, parts):
+        lhs = jnp.concatenate([parts[o], parts[o - 1], parts[o + 1]], axis=1)
+        return fold(jnp.dot(lhs, cw[o + 3], preferred_element_type=F32), nright, width)
 
     chip = me // 2
 
@@ -280,7 +329,7 @@
                 device_id=(member(ax, s),), device_id_type=MESH,
             ).wait_recv()
 
-    def gather_all(cyc, tile):
+    def gather_all(cyc, tile, between):
         gtile[cyc, 0] = tile
         pair = pltpu.make_async_remote_copy(
             src_ref=gtile.at[cyc, 0], dst_ref=gtile.at[cyc, 1],
@@ -301,6 +350,8 @@
             gather_waits(cyc, ax)
             for copy in copies:
                 copy.wait_send()
+            if ax == 0:
+                between()
         for c in range(64):
             pair_tile = gather[cyc, c]
             gfull[16 * c:16 * c + 8] = split_columns(pair_tile)
@@ -333,6 +384,7 @@
 
     halo_sent(jnp.int32(0))
     sweep(jnp.int32(0), None)
+    take_near()
 
     def cycle(cyc, _):
         n = 1 + 7 * cyc
@@ -370,39 +422,77 @@
         acc = lax.fori_loop(0, nrows // 8, restrict, jnp.zeros((2 * nright, width), F32))
         right_one = (acc[:nright] + acc[nright:]) * scale_one
 
-        m = 4 * cyc
-        it = RELAX * d1inv * right_one
-        it = it + RELAX * d1inv * (right_one - coarse_op(it, m))
-        resid_one = right_one - coarse_op(it, m + 1)
+        fbuf[cyc, 4] = right_one
+        for o in OFFSETS[:4]:
+            coarse_copy(cyc, o).start()
+        rate = {o: RELAX * small[o + 4, 0:1] for o in range(-4, 5)}
+        rhs_one, it, parts = {}, {}, {}
+
+        def first(o):
+            rhs_one[o] = fbuf[cyc, o + 4]
+            it[o] = rate[o] * rhs_one[o]
+            parts[o] = split(it[o])
+
+        def improve(offsets):
+            return {
+                o: it[o] + rate[o] * (rhs_one[o] - coarse_op(o, parts)) for o in offsets
+            }
+
+        first(0)
+        for o in OFFSETS[:4]:
+            coarse_copy(cyc, -o).wait_recv()
+            first(o)
+        second = improve((-1, 0, 1))
+        resid_one = rhs_one[0] - coarse_op(0, {o: split(second[o]) for o in second})
         padded = jnp.concatenate([resid_one, jnp.zeros((width - nright, width), F32)], axis=0)
         tile = lax.dot_general(
             table_two, padded, (((1,), (1,)), ((), ())),
             precision=lax.Precision.HIGHEST, preferred_element_type=F32,
         )
-        gather_all(cyc, tile)
-        e2 = fold(jnp.dot(inv_s[...], gfull[...], preferred_element_type=F32), 8, width)
-        e2t = jnp.concatenate([e2, jnp.zeros((width - 8, width), F32)], axis=0).T[:nright]
-        it = it + jnp.dot(
-            e2t, table_two_pad, precision=lax.Precision.HIGHEST, preferred_element_type=F32
-        )
-        it = it + RELAX * d1inv * (right_one - coarse_op(it, m + 2))
-        it = it + RELAX * d1inv * (right_one - coarse_op(it, m + 3))
-        cx[...] = split(it * scale_one)
+
+        def send_far():
+            for o in OFFSETS[4:]:
+                coarse_copy(cyc, o).start()
+
+        gather_all(cyc, tile, send_far)
+        e2 = fold(jnp.dot(inv_s[...], gfull[...], preferred_element_type=F32), 56, width)
+        e2t = split(
+            jnp.concatenate([e2, jnp.zeros((width - 56, width), F32)], axis=0).T[:nright]
+        )
+        for o in OFFSETS[4:]:
+            coarse_copy(cyc, -o).wait_recv()
+            first(o)
+        second.update(improve((-3, -2, 2, 3)))
+        it = {
+            o: second[o]
+            + fold(jnp.dot(e2t, tw[o + 3], preferred_element_type=F32), nright, width)
+            for o in second
+        }
+        parts = {o: split(it[o]) for o in it}
+        it = improve((-2, -1, 0, 1, 2))
+        parts = {o: split(it[o]) for o in it}
+        it = improve((-1, 0, 1))
+        for o in (-1, 0, 1):
+            cx[o + 1] = split(it[o] * small[o + 4, 1:2])
+        for o in OFFSETS:
+            coarse_copy(cyc, o).wait_send()
 
         n2 = n + 2
         par2 = lax.rem(n2, 2)
 
+        def lifted(value, hot):
+            res = jnp.dot(value, hot, preferred_element_type=F32)
+            return res[:nright] + res[nright:]
+
         def lift_row(j, fixed):
-            res = jnp.dot(cx[...], table[j], preferred_element_type=F32)
-            u = res[:nright] + res[nright:]
+            u = lifted(cx[1], table[j])
             u_ref[j] = u
-            publish(1 - par2, j, fixed, u)
+            publish(1 - par2, j, None, u)
 
         rows_first(lift_row)
-        halo_send(n2)
         rows_rest(lift_row)
-        halo_sent(n2)
-        halo_take(n2)
+        for m in range(8):
+            xs[par2, nrows + m] = split(lifted(cx[2 * (m // 4)], near_table[m]))
 
         def correct_row(j, fixed):
             d = SMOOTH * dinv[j]
@@ -452,7 +542,7 @@
             pltpu.VMEM(rhs_fields.shape, F32),
             pltpu.VMEM(diag_blocks.shape, F32),
             pltpu.VMEM(off_blocks.shape, F32),
-            pltpu.VMEM((8, coarse_inverse.shape[1]), F32),
+            pltpu.VMEM((7, 8, coarse_inverse.shape[1]), F32),
             pltpu.VMEM((nrows, 4 * width, 2 * width), BF16),
             pltpu.VMEM((2, nrows + 8, 2 * nright, width), BF16),
             pltpu.VMEM((nrows, nright, width), F32),
@@ -466,20 +556,28 @@
             pltpu.VMEM((8, nright, width), F32),
             pltpu.VMEM((3, 2, 4, nright, width), F32),
             pltpu.VMEM((3, 2, 4, nright, width), F32),
-            pltpu.VMEM((3 * width, 2 * width), BF16),
-            pltpu.VMEM((2 * nright, width), BF16),
-            pltpu.VMEM((3, nright, width), F32),
-            pltpu.VMEM((3, 2, nright, width), F32),
-            pltpu.VMEM((16, coarse_inverse.shape[1]), BF16),
+            pltpu.VMEM((7, 3 * width, 2 * width), BF16),
+            pltpu.VMEM((3, 2 * nright, width), BF16),
+            pltpu.VMEM((9, 16, width), F32),
+            pltpu.VMEM((7, width, width), F32),
+            pltpu.VMEM((7, 2, width, width), F32),
+            pltpu.VMEM((2, 9, nright, width), F32),
+            pltpu.VMEM((7, width, 2 * width), BF16),
+            pltpu.VMEM((8, width, width), BF16),
+            pltpu.VMEM((112, coarse_inverse.shape[1]), BF16),
             pltpu.VMEM((2, 2, 8, width), F32),
             pltpu.VMEM((2, 64, 8, width), F32),
             pltpu.VMEM((1024, 2 * width), BF16),
-            DMA((3,)),
+            DMA((9,)),
             DMA((nrows // CHUNK,)),
             DMA((3, 2)),
             DMA((3, 2)),
-            DMA((3, 2)),
-            DMA((3, 2)),
+            DMA((9,)),
+            DMA((9,)),
+            DMA((2, 7)),
+            DMA((2, 7)),
+            DMA((2, 9)),
+            DMA((2, 9)),
             DMA((2, 10)),
             DMA((2, 10)),
         ],

time: 192 us -> 165 us (0.86)
  Pallas kernels: 187 us -> 159 us
    pallas_call x1, Pallas kernels: 187 us -> 159 us  [local(): pl.pallas_call(kernel, name='multigrid', out_shape=jax.ShapeDtypeStruct(r...]
where the time goes in v2:
time: 165 us; the launch traced here: 164 us
  Pallas kernels  159 us (96%)
  local copies, waits for them, and re-layouts  5 us (3%)
    pallas_call x1, Pallas kernels, local(): pl.pallas_call(kernel, name='multigrid', out_shape=jax.ShapeDtypeStruct(r...  159 us

profile of v2, /device:TPU:0, one launch (start us, length us, event | category | flops | bytes accessed | tf_op | source)
XLA Modules:
  0.0 164.4 jit_solution(1951859081369387566)
XLA Ops:
  0.0 1.3 reshape.13.lists_in
  1.3 0.8 copy.12
  2.1 0.6 reshape.12.cols_in
  2.7 159.4 %multigrid.1 = f32[64,4096]{1,0:T(8,128)} custom-call(s32[96]{0:T(128)} %reshape.12.cols_in, s32[8]{0:T(128)} %reshape.13.lists_in, f32[64,4096]{1,0:T(8,128)} %rhs_hbm.1, f32[32,128,128]{2,1,0:T(8,128)} %diag_hbm.1, f32[32,3,128,128]{3,2,1,0:T(8,128)} %off_hbm.1, s32[32,1,128]{2,1,0:T(1,128)} %bitcast.2, f32[1,128,128]{2,1,0:T(8,128)} %cdiag_ref.1, ...), custom_call_target="tpu_custom_call" | custom-call | tf_op jit(solution)/shard_map/multigrid/pallas_call | solution.py:531
  162.1 2.3 %copy.14 = f32[64,4096]{1,0:T(8,128)} copy(f32[64,4096]{1,0:T(8,128)} %multigrid.1) | data formatting | bytes 2097152

commit v3 on v2

--- a/solution.py
+++ b/solution.py
@@ -11,6 +11,8 @@
 F32 = jnp.float32
 BF16 = jnp.bfloat16
 CHUNK = 4
+FIRST = 8
+GROUP = 24
 OFFSETS = (1, -1, 2, -2, 3, -3, 4, -4)
 
 
@@ -163,17 +165,20 @@
         )
         return fold(res, nright, width)
 
-    def rows_first(body):
-        for j in range(8):
-            body(j, j)
-
-    def rows_rest(body):
+    def rows_first(compute, store):
+        for g in range(0, 8, FIRST):
+            values = [compute(j) for j in range(g, g + FIRST)]
+            for u in range(FIRST):
+                store(g + u, g + u, values[u])
+
+    def rows_rest(compute, store):
         def step(g, _):
-            for u in range(8):
-                body(8 + g * 8 + u, None)
+            values = [compute(8 + g * GROUP + u) for u in range(GROUP)]
+            for u in range(GROUP):
+                store(8 + g * GROUP + u, None, values[u])
             return 0
 
-        lax.fori_loop(0, (nrows - 8) // 8, step, 0)
+        lax.fori_loop(0, (nrows - 8) // GROUP, step, 0)
 
     def publish(par, j, fixed, v):
         xs[1 - par, j] = split(v)
@@ -194,19 +199,21 @@
     for i in range(nrows):
         u_ref[i] = rhs_v[:, i * width:(i + 1) * width]
 
-    def start_row(j, fixed):
-        d = dnat[perm[j]]
+    def start_load(j):
+        return dnat[perm[j]], u_ref[perm[j]]
+
+    def start_row(j, fixed, value):
+        d, f = value
         dinv[j] = d
-        f = u_ref[perm[j]]
         f_ref[j] = f
         v = RELAX * d * f
         x_ref[j] = v
         publish(jnp.int32(1), j, fixed, v)
 
-    rows_first(start_row)
+    rows_first(start_load, start_row)
     pl.semaphore_wait(barrier, len(peers))
     halo_send(jnp.int32(0))
-    rows_rest(start_row)
+    rows_rest(start_load, start_row)
 
     def big_copies(o):
         return [
@@ -361,20 +368,22 @@
         par = lax.rem(n, 2)
         halo_take(n)
 
-        def body(j, fixed):
+        def relax(j):
             d = RELAX * dinv[j]
-            new = x_ref[j] + d * (f_ref[j] - product(par, j))
+            return x_ref[j] + d * (f_ref[j] - product(par, j))
+
+        def body(j, fixed, new):
             x_ref[j] = new
             publish(par, j, fixed, new)
 
-        rows_first(body)
+        rows_first(relax, body)
         if last is None:
             halo_send(n + 1)
         else:
             @pl.when(n < last)
             def _():
                 halo_send(n + 1)
-        rows_rest(body)
+        rows_rest(relax, body)
         if last is None:
             halo_sent(n + 1)
         else:
@@ -391,25 +400,30 @@
         par = lax.rem(n, 2)
         halo_take(n)
 
-        def resid_row(j, fixed):
-            r = f_ref[j] - product(par, j)
+        def resid(j):
+            return f_ref[j] - product(par, j)
+
+        def resid_row(j, fixed, r):
             r_ref[j] = r
             publish(par, j, fixed, dinv[j] * r)
 
-        rows_first(resid_row)
+        rows_first(resid, resid_row)
         halo_send(n + 1)
-        rows_rest(resid_row)
+        rows_rest(resid, resid_row)
         halo_sent(n + 1)
 
         n1 = n + 1
         par1 = lax.rem(n1, 2)
         halo_take(n1)
 
-        def smooth_row(j, fixed):
-            tbuf[j] = split(r_ref[j] - SMOOTH * product(par1, j))
-
-        rows_first(smooth_row)
-        rows_rest(smooth_row)
+        def smooth(j):
+            return r_ref[j] - SMOOTH * product(par1, j)
+
+        def smooth_row(j, fixed, t):
+            tbuf[j] = split(t)
+
+        rows_first(smooth, smooth_row)
+        rows_rest(smooth, smooth_row)
 
         def restrict(g, acc):
             for u in range(8):
@@ -484,25 +498,29 @@
             res = jnp.dot(value, hot, preferred_element_type=F32)
             return res[:nright] + res[nright:]
 
-        def lift_row(j, fixed):
-            u = lifted(cx[1], table[j])
+        def lift(j):
+            return lifted(cx[1], table[j])
+
+        def lift_row(j, fixed, u):
             u_ref[j] = u
             publish(1 - par2, j, None, u)
 
-        rows_first(lift_row)
-        rows_rest(lift_row)
+        rows_first(lift, lift_row)
+        rows_rest(lift, lift_row)
         for m in range(8):
             xs[par2, nrows + m] = split(lifted(cx[2 * (m // 4)], near_table[m]))
 
-        def correct_row(j, fixed):
+        def correct(j):
             d = SMOOTH * dinv[j]
-            new = x_ref[j] + u_ref[j] - d * product(par2, j)
+            return x_ref[j] + u_ref[j] - d * product(par2, j)
+
+        def correct_row(j, fixed, new):
             x_ref[j] = new
             publish(par2, j, fixed, new)
 
-        rows_first(correct_row)
+        rows_first(correct, correct_row)
         halo_send(n2 + 1)
-        rows_rest(correct_row)
+        rows_rest(correct, correct_row)
         halo_sent(n2 + 1)
 
         def sweeps(s, _):

time: 165 us -> 149 us (0.903)
  Pallas kernels: 159 us -> 144 us
    pallas_call x1, Pallas kernels: 159 us -> 144 us  [local(): pl.pallas_call(kernel, name='multigrid', out_shape=jax.ShapeDtypeStruct(r...]
where the time goes in v3:
time: 149 us
  Pallas kernels  144 us (97%)
  local copies, waits for them, and re-layouts  5 us (3%)
    pallas_call x1, Pallas kernels, local(): pl.pallas_call(kernel, name='multigrid', out_shape=jax.ShapeDtypeStruct(r...  144 us
    unnamed x2, local copies, waits for them, and re-layouts  3.03 us

profile of v3, /device:TPU:0, one launch (start us, length us, event | category | flops | bytes accessed | tf_op | source)
XLA Modules:
  0.0 148.6 jit_solution(4253908640873095194)
XLA Ops:
  0.0 1.3 reshape.13.lists_in
  1.3 0.8 copy.12
  2.1 0.6 reshape.12.cols_in
  2.7 143.6 %multigrid.1 = f32[64,4096]{1,0:T(8,128)} custom-call(s32[96]{0:T(128)} %reshape.12.cols_in, s32[8]{0:T(128)} %reshape.13.lists_in, f32[64,4096]{1,0:T(8,128)} %rhs_hbm.1, f32[32,128,128]{2,1,0:T(8,128)} %diag_hbm.1, f32[32,3,128,128]{3,2,1,0:T(8,128)} %off_hbm.1, s32[32,1,128]{2,1,0:T(1,128)} %bitcast.2, f32[1,128,128]{2,1,0:T(8,128)} %cdiag_ref.1, ...), custom_call_target="tpu_custom_call" | custom-call | tf_op jit(solution)/shard_map/multigrid/pallas_call | solution.py:549
  146.3 2.3 %copy.14 = f32[64,4096]{1,0:T(8,128)} copy(f32[64,4096]{1,0:T(8,128)} %multigrid.1) | data formatting | bytes 2097152

commit v4 on v3

--- a/solution.py
+++ b/solution.py
@@ -11,8 +11,7 @@
 F32 = jnp.float32
 BF16 = jnp.bfloat16
 CHUNK = 4
-FIRST = 8
-GROUP = 24
+GROUP = 16
 OFFSETS = (1, -1, 2, -2, 3, -3, 4, -4)
 
 
@@ -36,9 +35,8 @@
     cols_in, lists_in,
     rhs_hbm, diag_hbm, off_hbm, agg_ref, cdiag_ref, cside_ref, cagg_ref, inv_hbm,
     out_ref,
-    perm, pos, cols, sent_pos,
-    rhs_v, diag_v, off_v, inv_v, weights, xs, x_ref, r_ref, u_ref, f_ref, dnat, dinv, table, tbuf,
-    first8, send, recv, cw, cx, small, big_diag, big_side, fbuf, tw, near_table, inv_s,
+    rhs_v, diag_v, off_v, inv_v, weights, xs, x_ref, r_ref, u_ref, f_ref, dinv, table, tbuf,
+    send, recv, cw, cx, small, big_diag, big_side, fbuf, tw, near_table, inv_s,
     gtile, gather, gfull,
     load_sem, off_sem, send_sem, recv_sem, small_send, small_recv, big_send, big_recv,
     fsend_sem, frecv_sem, gsend_sem, grecv_sem,
@@ -92,98 +90,63 @@
 
     wanted = [lists_in[m] for m in range(8)]
 
-    def count_sent(i, total):
-        flag = wanted[0] == i
-        for m in range(1, 8):
-            flag = jnp.logical_or(flag, wanted[m] == i)
-        value = flag.astype(jnp.int32)
-        pos[i] = value
-        return total + value
-
-    nsent = lax.fori_loop(0, nrows, count_sent, jnp.int32(0))
-
-    def place(i, carry):
-        a, b = carry
-        value = pos[i]
-        pos[i] = jnp.where(value == 1, a, b)
-        return a + value, b + 1 - value
-
-    lax.fori_loop(0, nrows, place, (jnp.int32(0), nsent))
-
-    def invert(j, _):
-        total = jnp.int32(0)
-        for i in range(nrows):
-            total = total + jnp.where(pos[i] == j, i, 0)
-        perm[j] = total
-        for k in range(3):
-            c = cols_in[total * 3 + k]
-            own = pos[jnp.minimum(c, nrows - 1)]
-            cols[j * 3 + k] = jnp.where(c < nrows, own, c)
-        return 0
-
-    lax.fori_loop(0, nrows, invert, 0)
-    for m in range(8):
-        sent_pos[m] = pos[wanted[m]]
-
-    def halo_copies(n):
+    def halo_copies(n, h):
         slot = lax.rem(n, 3)
+        half = pl.ds(2 * h, 2)
         up = pltpu.make_async_remote_copy(
-            src_ref=send.at[slot, 1], dst_ref=recv.at[slot, 0],
-            send_sem=send_sem.at[slot, 1], recv_sem=recv_sem.at[slot, 0],
+            src_ref=send.at[slot, 1, half], dst_ref=recv.at[slot, 0, half],
+            send_sem=send_sem.at[slot, 1, h], recv_sem=recv_sem.at[slot, 0, h],
             device_id=(upper,), device_id_type=MESH,
         )
         down = pltpu.make_async_remote_copy(
-            src_ref=send.at[slot, 0], dst_ref=recv.at[slot, 1],
-            send_sem=send_sem.at[slot, 0], recv_sem=recv_sem.at[slot, 1],
+            src_ref=send.at[slot, 0, half], dst_ref=recv.at[slot, 1, half],
+            send_sem=send_sem.at[slot, 0, h], recv_sem=recv_sem.at[slot, 1, h],
             device_id=(lower,), device_id_type=MESH,
         )
         return up, down
 
-    def halo_send(n):
+    def halo_send(n, value):
         slot = lax.rem(n, 3)
-        for m in range(8):
-            send[slot, m // 4, m % 4] = first8[sent_pos[m]]
-        up, down = halo_copies(n)
-        up.start()
-        down.start()
+        for h in range(2):
+            places = [(side, 2 * h + q) for q in range(2) for side in range(2)]
+            values = [value(wanted[4 * side + q]) for side, q in places]
+            for (side, q), v in zip(places, values):
+                send[slot, side, q] = v
+            for copy in halo_copies(n, h):
+                copy.start()
 
     def halo_sent(n):
-        for copy in halo_copies(n):
-            copy.wait_send()
+        for h in range(2):
+            for copy in halo_copies(n, h):
+                copy.wait_send()
 
     def halo_take(n):
         slot, par = lax.rem(n, 3), lax.rem(n, 2)
-        for copy in halo_copies(n):
-            copy.wait_recv()
-        for m in range(8):
-            xs[par, nrows + m] = split(recv[slot, m // 4, m % 4])
+        for h in range(2):
+            for copy in halo_copies(n, h):
+                copy.wait_recv()
+            for q in range(2 * h, 2 * h + 2):
+                for side in range(2):
+                    xs[par, nrows + 4 * side + q] = split(recv[slot, side, q])
 
     def product(par, j):
-        parts = [xs[par, j]] + [xs[par, cols[j * 3 + k]] for k in range(3)]
+        parts = [xs[par, j]] + [xs[par, cols_in[j * 3 + k]] for k in range(3)]
         res = jnp.dot(
-            jnp.concatenate(parts, axis=1), weights[perm[j]], preferred_element_type=F32
+            jnp.concatenate(parts, axis=1), weights[j], preferred_element_type=F32
         )
         return fold(res, nright, width)
 
-    def rows_first(compute, store):
-        for g in range(0, 8, FIRST):
-            values = [compute(j) for j in range(g, g + FIRST)]
-            for u in range(FIRST):
-                store(g + u, g + u, values[u])
-
-    def rows_rest(compute, store):
+    def rows(compute, store):
         def step(g, _):
-            values = [compute(8 + g * GROUP + u) for u in range(GROUP)]
+            values = [compute(g * GROUP + u) for u in range(GROUP)]
             for u in range(GROUP):
-                store(8 + g * GROUP + u, None, values[u])
+                store(g * GROUP + u, values[u])
             return 0
 
-        lax.fori_loop(0, (nrows - 8) // GROUP, step, 0)
-
-    def publish(par, j, fixed, v):
+        lax.fori_loop(0, nrows // GROUP, step, 0)
+
+    def publish(par, j, v):
         xs[1 - par, j] = split(v)
-        if fixed is not None:
-            first8[fixed] = v
 
     rows_iota = lax.broadcasted_iota(jnp.int32, (width, width), 0)
     eye = rows_iota == lax.broadcasted_iota(jnp.int32, (width, width), 1)
@@ -191,29 +154,22 @@
 
     def take_diag(i, _):
         d = jnp.sum(jnp.where(eye, diag_v[i], 0.0), axis=0, keepdims=True)
-        dnat[i] = 1.0 / d
+        dinv[i] = 1.0 / d
         return 0
 
     lax.fori_loop(0, nrows, take_diag, 0)
     load_rhs.wait()
     for i in range(nrows):
-        u_ref[i] = rhs_v[:, i * width:(i + 1) * width]
-
-    def start_load(j):
-        return dnat[perm[j]], u_ref[perm[j]]
-
-    def start_row(j, fixed, value):
-        d, f = value
-        dinv[j] = d
-        f_ref[j] = f
-        v = RELAX * d * f
+        f_ref[i] = rhs_v[:, i * width:(i + 1) * width]
+
+    pl.semaphore_wait(barrier, len(peers))
+    halo_send(jnp.int32(0), lambda q: RELAX * dinv[q] * f_ref[q])
+
+    def start_row(j, v):
         x_ref[j] = v
-        publish(jnp.int32(1), j, fixed, v)
-
-    rows_first(start_load, start_row)
-    pl.semaphore_wait(barrier, len(peers))
-    halo_send(jnp.int32(0))
-    rows_rest(start_load, start_row)
+        publish(jnp.int32(1), j, v)
+
+    rows(lambda j: RELAX * dinv[j] * f_ref[j], start_row)
 
     def big_copies(o):
         return [
@@ -243,7 +199,7 @@
     lax.fori_loop(0, nrows // CHUNK, convert, 0)
 
     def make_table(j, sums):
-        hot = (agg_ref[perm[j]] == rows_iota).astype(F32)
+        hot = (agg_ref[j] == rows_iota).astype(F32)
         table[j] = hot.astype(BF16)
         return sums + hot
 
@@ -372,18 +328,17 @@
             d = RELAX * dinv[j]
             return x_ref[j] + d * (f_ref[j] - product(par, j))
 
-        def body(j, fixed, new):
+        def body(j, new):
             x_ref[j] = new
-            publish(par, j, fixed, new)
-
-        rows_first(relax, body)
+            publish(par, j, new)
+
         if last is None:
-            halo_send(n + 1)
+            halo_send(n + 1, relax)
         else:
             @pl.when(n < last)
             def _():
-                halo_send(n + 1)
-        rows_rest(relax, body)
+                halo_send(n + 1, relax)
+        rows(relax, body)
         if last is None:
             halo_sent(n + 1)
         else:
@@ -403,13 +358,12 @@
         def resid(j):
             return f_ref[j] - product(par, j)
 
-        def resid_row(j, fixed, r):
+        def resid_row(j, r):
             r_ref[j] = r
-            publish(par, j, fixed, dinv[j] * r)
-
-        rows_first(resid, resid_row)
-        halo_send(n + 1)
-        rows_rest(resid, resid_row)
+            publish(par, j, dinv[j] * r)
+
+        halo_send(n + 1, lambda q: dinv[q] * resid(q))
+        rows(resid, resid_row)
         halo_sent(n + 1)
 
         n1 = n + 1
@@ -419,11 +373,10 @@
         def smooth(j):
             return r_ref[j] - SMOOTH * product(par1, j)
 
-        def smooth_row(j, fixed, t):
+        def smooth_row(j, t):
             tbuf[j] = split(t)
 
-        rows_first(smooth, smooth_row)
-        rows_rest(smooth, smooth_row)
+        rows(smooth, smooth_row)
 
         def restrict(g, acc):
             for u in range(8):
@@ -501,12 +454,11 @@
         def lift(j):
             return lifted(cx[1], table[j])
 
-        def lift_row(j, fixed, u):
+        def lift_row(j, u):
             u_ref[j] = u
-            publish(1 - par2, j, None, u)
-
-        rows_first(lift, lift_row)
-        rows_rest(lift, lift_row)
+            publish(1 - par2, j, u)
+
+        rows(lift, lift_row)
         for m in range(8):
             xs[par2, nrows + m] = split(lifted(cx[2 * (m // 4)], near_table[m]))
 
@@ -514,13 +466,12 @@
             d = SMOOTH * dinv[j]
             return x_ref[j] + u_ref[j] - d * product(par2, j)
 
-        def correct_row(j, fixed, new):
+        def correct_row(j, new):
             x_ref[j] = new
-            publish(par2, j, fixed, new)
-
-        rows_first(correct, correct_row)
-        halo_send(n2 + 1)
-        rows_rest(correct, correct_row)
+            publish(par2, j, new)
+
+        halo_send(n2 + 1, correct)
+        rows(correct, correct_row)
         halo_sent(n2 + 1)
 
         def sweeps(s, _):
@@ -532,7 +483,7 @@
 
     lax.fori_loop(0, 2, cycle, 0)
     for i in range(nrows):
-        out_ref[:, i * width:(i + 1) * width] = x_ref[pos[i]]
+        out_ref[:, i * width:(i + 1) * width] = x_ref[i]
 
 
 def local(
@@ -553,10 +504,6 @@
         in_specs=[S, S, A, A, A, V, V, V, V, A],
         out_specs=V,
         scratch_shapes=[
-            pltpu.SMEM((nrows,), jnp.int32),
-            pltpu.SMEM((nrows,), jnp.int32),
-            pltpu.SMEM((3 * nrows,), jnp.int32),
-            pltpu.SMEM((8,), jnp.int32),
             pltpu.VMEM(rhs_fields.shape, F32),
             pltpu.VMEM(diag_blocks.shape, F32),
             pltpu.VMEM(off_blocks.shape, F32),
@@ -568,10 +515,8 @@
             pltpu.VMEM((nrows, nright, width), F32),
             pltpu.VMEM((nrows, nright, width), F32),
             pltpu.VMEM((nrows, 1, width), F32),
-            pltpu.VMEM((nrows, 1, width), F32),
             pltpu.VMEM((nrows, naggs, width), BF16),
             pltpu.VMEM((nrows, 2 * nright, width), BF16),
-            pltpu.VMEM((8, nright, width), F32),
             pltpu.VMEM((3, 2, 4, nright, width), F32),
             pltpu.VMEM((3, 2, 4, nright, width), F32),
             pltpu.VMEM((7, 3 * width, 2 * width), BF16),
@@ -588,8 +533,8 @@
             pltpu.VMEM((1024, 2 * width), BF16),
             DMA((9,)),
             DMA((nrows // CHUNK,)),
-            DMA((3, 2)),
-            DMA((3, 2)),
+            DMA((3, 2, 2)),
+            DMA((3, 2, 2)),
             DMA((9,)),
             DMA((9,)),
             DMA((2, 7)),

time: 149 us -> 148 us (level)
  no operation moved by 1% of the time
where the time goes in v4:
time: 148 us
  Pallas kernels  143 us (97%)
  local copies, waits for them, and re-layouts  5 us (3%)
    pallas_call x1, Pallas kernels, local(): pl.pallas_call(kernel, name='multigrid', out_shape=jax.ShapeDtypeStruct(r...  143 us
    unnamed x2, local copies, waits for them, and re-layouts  3.03 us

profile of v4, /device:TPU:0, one launch (start us, length us, event | category | flops | bytes accessed | tf_op | source)
XLA Modules:
  0.0 147.8 jit_solution(14767425437348866676)
XLA Ops:
  0.0 1.3 reshape.13.lists_in
  1.3 0.8 copy.12
  2.1 0.6 reshape.12.cols_in
  2.7 142.8 %multigrid.1 = f32[64,4096]{1,0:T(8,128)} custom-call(s32[96]{0:T(128)} %reshape.12.cols_in, s32[8]{0:T(128)} %reshape.13.lists_in, f32[64,4096]{1,0:T(8,128)} %rhs_hbm.1, f32[32,128,128]{2,1,0:T(8,128)} %diag_hbm.1, f32[32,3,128,128]{3,2,1,0:T(8,128)} %off_hbm.1, s32[32,1,128]{2,1,0:T(1,128)} %bitcast.2, f32[1,128,128]{2,1,0:T(8,128)} %cdiag_ref.1, ...), custom_call_target="tpu_custom_call" | custom-call | tf_op jit(solution)/shard_map/multigrid/pallas_call | solution.py:500
  145.5 2.3 %copy.14 = f32[64,4096]{1,0:T(8,128)} copy(f32[64,4096]{1,0:T(8,128)} %multigrid.1) | data formatting | bytes 2097152

commit v5 on v4

--- a/solution.py
+++ b/solution.py
@@ -11,7 +11,7 @@
 F32 = jnp.float32
 BF16 = jnp.bfloat16
 CHUNK = 4
-GROUP = 16
+GROUP = 32
 OFFSETS = (1, -1, 2, -2, 3, -3, 4, -4)
 
 

time: 148 us -> 147 us (level)
  no operation moved by 1% of the time
where the time goes in v5:
time: 147 us
  Pallas kernels  142 us (97%)
  local copies, waits for them, and re-layouts  5 us (3%)
    pallas_call x1, Pallas kernels, local(): pl.pallas_call(kernel, name='multigrid', out_shape=jax.ShapeDtypeStruct(r...  142 us
    unnamed x2, local copies, waits for them, and re-layouts  3.03 us

profile of v5, /device:TPU:0, one launch (start us, length us, event | category | flops | bytes accessed | tf_op | source)
XLA Modules:
  0.0 146.6 jit_solution(13523274564048222430)
XLA Ops:
  0.0 1.3 reshape.13.lists_in
  1.3 0.8 copy.12
  2.1 0.6 reshape.12.cols_in
  2.7 141.6 %multigrid.1 = f32[64,4096]{1,0:T(8,128)} custom-call(s32[96]{0:T(128)} %reshape.12.cols_in, s32[8]{0:T(128)} %reshape.13.lists_in, f32[64,4096]{1,0:T(8,128)} %rhs_hbm.1, f32[32,128,128]{2,1,0:T(8,128)} %diag_hbm.1, f32[32,3,128,128]{3,2,1,0:T(8,128)} %off_hbm.1, s32[32,1,128]{2,1,0:T(1,128)} %bitcast.2, f32[1,128,128]{2,1,0:T(8,128)} %cdiag_ref.1, ...), custom_call_target="tpu_custom_call" | custom-call | tf_op jit(solution)/shard_map/multigrid/pallas_call | solution.py:500
  144.4 2.3 %copy.14 = f32[64,4096]{1,0:T(8,128)} copy(f32[64,4096]{1,0:T(8,128)} %multigrid.1) | data formatting | bytes 2097152
